TPU v7x, 32 devices: a whole 2x2x4 slice. The times are simulated.
32 devices in a mesh: donor: 16 (over z, y, x), gene: 2 (over core).
Axes of the slice: x: 2, y: 2, z: 4, core: 2. Of those that a mesh axis runs over, the one named last changes fastest.
Arguments:
- embeddings: bfloat16 [32768, 512], P('donor', 'gene')
- targets_by_gene: bfloat16 [5120, 32768], P(('gene', 'donor')), may hold values from -6 to 6
- cell_counts: int32 [16], P('donor'), may hold values from 1024 to 2048, as said below
Outputs:
- coefficients: float32 [512, 5120], P('donor', 'gene')
Inputs may be any that keep to these rules, and one draw needn't show every extreme that they name: `cell_counts`: every entry is a multiple of 128; some entry equals 2048 and some entry equals 2048/2.
All inputs are finite; a program needn't handle non-finite values.
Results may differ from a plain program's by a relative error of at most 0.0003.
Values may be sent and summed in bfloat16 or wider, within the bound.
No kernel may reach another device: no remote copies, remote signals or barrier semaphores. Data moves between devices by JAX's collectives and lax.ppermute only.
A program may use at most 128 MiB of HBM per device.

v0:
```python
import math
import jax
import jax.numpy as jnp
from jax import lax
from jax.sharding import PartitionSpec as P


def solve_both(lower_factor, right_cols):
    halfway = lax.linalg.triangular_solve(lower_factor, right_cols, left_side=True, lower=True)
    return lax.linalg.triangular_solve(
        lower_factor, halfway, left_side=True, lower=True, transpose_a=True
    )


def shards(embeddings, targets_by_gene, cell_counts):
    valid_count = cell_counts[0]
    gathered = lax.all_gather(embeddings, "gene", axis=1, tiled=True)
    row_total = gathered.shape[0]
    width = gathered.shape[1]
    donors = lax.axis_size("donor")
    row_valid = lax.broadcasted_iota(jnp.int32, (row_total, 1), 0) < valid_count
    masked = jnp.where(row_valid, gathered, jnp.zeros_like(gathered))
    gram_matrix = lax.dot_general(
        masked, masked, (((0,), (0,)), ((), ())), preferred_element_type=jnp.float32
    )
    by_rows = lax.all_to_all(targets_by_gene, "donor", split_axis=1, concat_axis=0, tiled=True)
    gram_matrix = lax.psum(gram_matrix, "donor")
    lower_factor = jnp.linalg.cholesky(gram_matrix)
    scale_total = math.sqrt(row_total * donors)
    cross_local = jnp.dot(by_rows, masked, preferred_element_type=jnp.float32)
    cross_sum = lax.psum(cross_local, "donor")
    scaled = scale_total * solve_both(lower_factor, cross_sum.T)
    share = width // donors
    first_row = lax.axis_index("donor") * share
    return lax.dynamic_slice_in_dim(scaled, first_row, share, 0)


def solution(mesh):
    placed = (P("donor", "gene"), P(("gene", "donor"), None), P("donor"))
    return jax.shard_map(
        shards, mesh=mesh, in_specs=placed, out_specs=P("donor", "gene"), check_vma=False
    )
```

profile of v0, /device:TPU:0, one launch (start us, length us, event | category | flops | bytes accessed | tf_op | source)
XLA Modules:
  0.0 653.4 jit_solution(13016904788041452031)
XLA Ops:
  6.5 10.0 %copy.17 = bf16[20,16,8,2048]{3,2,0,1:T(8,128)(2,1)} copy(bf16[20,16,8,2048]{3,2,1,0:T(8,128)(2,1)} %bitcast.68) | data formatting | bytes 20971520 | tf_op jit(solution)/shard_map/all_to_all | solution.py:26
  16.6 8.4 %all-to-all-start = ((bf16[160,16,2048]{2,0,1:T(8,128)(2,1)}), bf16[160,16,2048]{2,0,1:T(8,128)(2,1)}, u32[]{:S(2)}, u32[]{:S(2)}) async-start(bf16[160,16,2048]{2,0,1:T(8,128)(2,1)} %bitcast.67), calls=%async_computation | async-start | bytes 20971520 | tf_op jit(solution)/shard_map/all_to_all | solution.py:26
  24.9 0.0 all-gather.2.cloned.1.call-start
  25.0 0.7 all-gather.2.cloned.1.call-update
  25.7 0.0 all-reduce.4.cloned.1.call-start
  26.4 12.5 %all-gather.2.cloned.1.call-done = bf16[2048,512]{1,0:T(8,128)(2,1)} async-done(((bf16[2048,256]{1,0:T(8,128)(2,1)}), bf16[2048,512]{1,0:T(8,128)(2,1)}) %all-gather.2.cloned.1.call-update) | async-done | bytes 2097168 | tf_op jit(solution)/shard_map/all_gather | solution.py:17
  38.9 5.2 fusion.28
  44.1 178.5 %all-to-all-done = bf16[160,16,2048]{2,0,1:T(8,128)(2,1)} async-done(((bf16[160,16,2048]{2,0,1:T(8,128)(2,1)}), bf16[160,16,2048]{2,0,1:T(8,128)(2,1)}, u32[]{:S(2)}, u32[]{:S(2)}) %all-to-all-start) | async-done | bytes 10485792 | tf_op jit(solution)/shard_map/all_to_all | solution.py:26
  222.6 10.8 %fusion.27 = f32[512,2560]{1,0:T(8,128)} fusion(bf16[2560,2048]{1,0:T(8,128)(2,1)} %bitcast.10, bf16[2048,512]{1,0:T(8,128)(2,1)S(1)} %copy-done.1, pred[2048]{0:T(1024)(128)(4,1)S(1)} %iota_compare_fusion.3), kind=kOutput, calls=%fused_computation.43 | convolution fusion | flops 5369757696 | bytes 17827840 | tf_op jit(solution)/shard_map/dot_general | solution.py:30
  233.4 0.0 all-reduce.4.cloned.1.call-update
  233.5 251.7 %all-reduce.4.cloned.1.call-done = (f32[512,2560]{1,0:T(8,128)}, f32[512,512]{0,1:T(8,128)}) async-done(((f32[512,2560]{1,0:T(8,128)}, f32[512,512]{0,1:T(8,128)}), (f32[512,2560]{1,0:T(8,128)}, f32[512,512]{0,1:T(8,128)})) %all-reduce.4.cloned.1.call-update) | async-done | bytes 6291472 | tf_op jit(solution)/shard_map/psum | solution.py:31
  485.2 1.6 copy.12
  486.8 0.0 copy-done
  486.8 0.2 fusion.26
  487.1 11.7 %cholesky.104 = f32[128,128]{1,0:T(8,128)S(1)} custom-call(f32[128,128]{1,0:T(8,128)S(1)} %cholesky.266), custom_call_target="Cholesky" | custom-call | tf_op jit(solution)/shard_map/jit(cholesky)/cholesky | solution.py:28
  498.8 0.1 cholesky.224
  498.9 9.8 %custom-call.32 = f32[1,128,128]{1,2,0:T(8,128)S(1)} custom-call(f32[1,128,128]{2,1,0:T(8,128)S(1)} %get-tuple-element.34), custom_call_target="InvertDiagBlocksLowerTriangular" | custom-call | tf_op jit(solution)/shard_map/jit(cholesky)/cholesky | solution.py:28
  508.8 0.3 constant_dynamic-update-slice_fusion
  509.1 0.3 convolution_subtract_fusion.4
  509.4 11.7 %cholesky.217 = f32[128,128]{1,0:T(8,128)S(1)} custom-call(f32[128,128]{1,0:T(8,128)S(1)} %cholesky.270), custom_call_target="Cholesky" | custom-call | tf_op jit(solution)/shard_map/jit(cholesky)/cholesky | solution.py:28
  521.2 10.2 %custom-call.33 = f32[1,128,128]{1,2,0:T(8,128)S(1)} custom-call(f32[1,128,128]{2,1,0:T(8,128)S(1)} %get-tuple-element.31), custom_call_target="InvertDiagBlocksLowerTriangular" | custom-call | tf_op jit(solution)/shard_map/jit(cholesky)/cholesky | solution.py:28
  531.4 0.3 convolution_dynamic-update-slice_fusion
  531.6 0.0 slice-start
  531.6 0.4 convolution_subtract_fusion.5
  532.0 11.7 %cholesky.238 = f32[128,128]{1,0:T(8,128)S(1)} custom-call(f32[128,128]{1,0:T(8,128)S(1)} %cholesky.275), custom_call_target="Cholesky" | custom-call | tf_op jit(solution)/shard_map/jit(cholesky)/cholesky | solution.py:28
  543.8 9.8 %custom-call.34 = f32[1,128,128]{1,2,0:T(8,128)S(1)} custom-call(f32[1,128,128]{2,1,0:T(8,128)S(1)} %get-tuple-element.28), custom_call_target="InvertDiagBlocksLowerTriangular" | custom-call | tf_op jit(solution)/shard_map/jit(cholesky)/cholesky | solution.py:28
  553.6 0.2 convolution_dynamic-update-slice_fusion.1
  553.8 0.4 convolution_subtract_fusion.6
  554.2 11.7 %cholesky.255 = f32[128,128]{1,0:T(8,128)S(1)} custom-call(f32[128,128]{1,0:T(8,128)S(1)} %convolution_subtract_fusion.6), custom_call_target="Cholesky" | custom-call | tf_op jit(solution)/shard_map/jit(cholesky)/cholesky | solution.py:28
  566.0 0.7 compare_reduce_fusion.1
  566.6 0.7 compare_reduce_fusion
  567.3 0.7 compare_reduce_fusion.2
  570.6 0.3 select_select_fusion
  570.9 10.6 %while.1 = (s32[]{:T(128)}, f32[512,512]{1,0:T(8,128)S(1)}, s32[4,2]{0,1:T(2,128)S(1)}, f32[4,128,128]{2,1,0:T(8,128)}, s32[]{:T(128)}) while((s32[]{:T(128)}, f32[512,512]{1,0:T(8,128)S(1)}, s32[4,2]{0,1:T(2,128)S(1)}, f32[4,128,128]{2,1,0:T(8,128)}, s32[]{:T(128)}) %tuple.27), condition=%wide.while_cond, body=%wide.while_body.sunk | while | flops 2 | bytes 132205 | solution.py:10
  570.9 0.1 constant_dynamic-slice_fusion.2
  571.0 0.6 fusion.76
  571.6 2.0 bitcast_dynamic-update-slice_fusion.2
  573.5 0.1 constant_dynamic-slice_fusion.2
  573.6 0.6 fusion.76
  574.2 2.0 bitcast_dynamic-update-slice_fusion.2
  576.2 0.1 constant_dynamic-slice_fusion.2
  576.3 0.6 fusion.76
  576.8 2.0 bitcast_dynamic-update-slice_fusion.2
  578.8 0.1 constant_dynamic-slice_fusion.2
  578.9 0.6 fusion.76
  579.5 2.0 bitcast_dynamic-update-slice_fusion.2
  581.5 40.1 %custom-call.35 = f32[4,128,128]{1,2,0:T(8,128)S(1)} custom-call(f32[4,128,128]{2,1,0:T(8,128)} %get-tuple-element.12), custom_call_target="InvertDiagBlocksLowerTriangular" | custom-call | tf_op jit(solution)/shard_map/triangular_solve | solution.py:10
  621.6 0.0 slice-start.1
  621.6 2.7 fusion.24
  624.3 2.6 convolution_subtract_fusion.1
  626.9 1.3 fusion.52
  628.2 0.0 slice-done
  628.2 1.5 convolution_subtract_fusion.3
  629.8 1.3 fusion.54
  631.0 2.5 fusion.15
  633.5 1.3 fusion.56
  634.8 1.3 fusion.55
  636.1 1.5 convolution_subtract_fusion
  637.6 1.3 fusion.53
  638.9 1.6 convolution_subtract_fusion.2
  640.4 1.3 fusion.51
  641.7 2.5 fusion.12
  644.2 1.3 fusion.50
  645.5 0.8 fusion.32
  (16 shorter events, 0.2 us)
Async XLA Ops:
  16.6 206.0 %all-to-all-start = ((bf16[160,16,2048]{2,0,1:T(8,128)(2,1)}), bf16[160,16,2048]{2,0,1:T(8,128)(2,1)}, u32[]{:S(2)}, u32[]{:S(2)}) async-start(bf16[160,16,2048]{2,0,1:T(8,128)(2,1)} %bitcast.67), calls=%async_computation | async-start | bytes 20971520 | tf_op jit(solution)/shard_map/all_to_all | solution.py:26
  24.9 14.0 %all-gather.2.cloned.1.call-start = ((), (), s32[]{:S(2)}) async-start(), calls=%async_computation.1 | async-start | bytes 3145728 | tf_op jit(solution)/shard_map/all_gather | solution.py:17
  25.7 459.5 %all-reduce.4.cloned.1.call-start = ((), (), s32[]{:S(2)}) async-start(), calls=%async_computation.2 | async-start | bytes 12582912 | tf_op jit(solution)/shard_map/psum | solution.py:31
  38.9 183.7 %copy-start.1 = (bf16[2048,512]{1,0:T(8,128)(2,1)S(1)}, bf16[2048,512]{1,0:T(8,128)(2,1)}, u32[]{:S(2)}) copy-start(bf16[2048,512]{1,0:T(8,128)(2,1)} %all-gather.2.cloned.1.call-done) | copy-start | bytes 6291460
  485.2 1.7 copy-start
  531.6 96.5 %slice-start = ((s8[5242880]{0:T(1024)(128)(4,1)}), s8[1048576]{0:T(1024)(128)(4,1)S(1)}, s32[]{:S(2)}) async-start(s8[5242880]{0:T(1024)(128)(4,1)} %bitcast.69), calls=%async_computation.3 | async-start | bytes 2097152
  621.6 6.6 %slice-start.1 = ((s8[5242880]{0:T(1024)(128)(4,1)}), s8[4194304]{0:T(1024)(128)(4,1)S(1)}, s32[]{:S(2)}) async-start(s8[5242880]{0:T(1024)(128)(4,1)} %bitcast.69), calls=%async_computation.4 | async-start | bytes 8388608
Sparse Core Ops, SparseCore 0:
  27.3 11.5 all-gather.1
  233.6 251.5 all-reduce.3
where the time goes:
time: 659 us; the launch traced here: 653 us
  waiting for transfers between devices  443 us (67%)
  other arithmetic  120 us (18%)
  matrix products  41.6 us (6%)
  local copies, waits for them, and re-layouts  22.4 us (3%)
  between operations  17.2 us (3%)
  starting transfers between devices  8.44 us (1%)
    psum x1, waiting for transfers between devices, shards(): cross_sum = lax.psum(cross_local, 'donor')  252 us
    all_to_all x1, waiting for transfers between devices, shards(): lax.all_to_all(targets_by_gene, 'donor', split_axis=1, concat_axis=0, til...  178 us
    another operation x14, other arithmetic, shards(): lower_factor = jnp.linalg.cholesky(gram_matrix)  78.9 us
    another operation x3, other arithmetic, solve_both(): lax.linalg.triangular_solve(lower_factor, halfway, left_side=True, lower=...  40.4 us
  transfers between devices with their start and end apart: 3, of which 3 were waited for; matrix products, arithmetic and copies ran while one was open for 1% of the time, Pallas kernels for 0%

commit v1 on v0

--- a/solution.py
+++ b/solution.py
@@ -28,7 +28,11 @@
     lower_factor = jnp.linalg.cholesky(gram_matrix)
     scale_total = math.sqrt(row_total * donors)
     cross_local = jnp.dot(by_rows, masked, preferred_element_type=jnp.float32)
-    cross_sum = lax.psum(cross_local, "donor")
+    cross_sum = cross_local
+    for hop in (1, 2, 4, 8):
+        cross_sum = cross_sum + lax.ppermute(
+            cross_sum, "donor", [(dev, dev ^ hop) for dev in range(16)]
+        )
     scaled = scale_total * solve_both(lower_factor, cross_sum.T)
     share = width // donors
     first_row = lax.axis_index("donor") * share

time: 659 us -> 910 us (1.38)
  waiting for transfers between devices: 443 us -> 641 us
  starting transfers between devices: 8.44 us -> 55.4 us
  other arithmetic: 120 us -> 136 us
    ppermute x0 -> x4, waiting for transfers between devices: none -> 444 us  [shards(): lax.ppermute(cross_sum, 'donor', [(dev, dev ^ hop) for dev in range(16)])]
    psum x1, waiting for transfers between devices: 252 us -> 0.01 us  [shards(): gram_matrix = lax.psum(gram_matrix, 'donor')]
    ppermute x0 -> x4, starting transfers between devices: none -> 46.9 us  [shards(): lax.ppermute(cross_sum, 'donor', [(dev, dev ^ hop) for dev in range(16)])]
    add x0 -> x3, other arithmetic: none -> 11.6 us  [shards(): cross_sum + lax.ppermute(cross_sum, 'donor', [(dev, dev ^ hop) for dev in...]
  transfers between devices with their start and end apart: 3 -> 7, of which waited for: 3 -> 6; matrix products, arithmetic and copies ran while one was open for 1% -> 16% of each run, Pallas kernels for 0% -> 0%
where the time goes in v1:
time: 910 us; the launch traced here: 905 us
  waiting for transfers between devices  641 us (70%)
  other arithmetic  136 us (15%)
  starting transfers between devices  55.4 us (6%)
  matrix products  35.7 us (4%)
  local copies, waits for them, and re-layouts  19.7 us (2%)
  between operations  17.2 us (2%)
    ppermute x4, waiting for transfers between devices, shards(): lax.ppermute(cross_sum, 'donor', [(dev, dev ^ hop) for dev in range(16)])  444 us
    all_to_all x1, waiting for transfers between devices, shards(): lax.all_to_all(targets_by_gene, 'donor', split_axis=1, concat_axis=0, til...  184 us
    another operation x14, other arithmetic, shards(): lower_factor = jnp.linalg.cholesky(gram_matrix)  78.9 us
    ppermute x4, starting transfers between devices, shards(): lax.ppermute(cross_sum, 'donor', [(dev, dev ^ hop) for dev in range(16)])  46.9 us
    another operation x3, other arithmetic, solve_both(): lax.linalg.triangular_solve(lower_factor, halfway, left_side=True, lower=...  39.6 us
  transfers between devices with their start and end apart: 7, of which 6 were waited for; matrix products, arithmetic and copies ran while one was open for 16% of the time, Pallas kernels for 0%

profile of v1, /device:TPU:0, one launch (start us, length us, event | category | flops | bytes accessed | tf_op | source)
XLA Modules:
  0.0 905.2 jit_solution(3618072949997934989)
XLA Ops:
  6.5 10.0 %copy.17 = bf16[20,16,8,2048]{3,2,0,1:T(8,128)(2,1)} copy(bf16[20,16,8,2048]{3,2,1,0:T(8,128)(2,1)} %bitcast.69) | data formatting | bytes 20971520 | tf_op jit(solution)/shard_map/all_to_all | solution.py:26
  16.6 8.4 all-to-all-start
  25.0 0.7 all-gather.2.cloned.1.call-update
  26.4 12.5 %all-gather.2.cloned.1.call-done = bf16[2048,512]{1,0:T(8,128)(2,1)} async-done(((bf16[2048,256]{1,0:T(8,128)(2,1)}), bf16[2048,512]{1,0:T(8,128)(2,1)}) %all-gather.2.cloned.1.call-update) | async-done | bytes 2097168 | tf_op jit(solution)/shard_map/all_gather | solution.py:17
  38.9 183.7 %all-to-all-done = bf16[160,16,2048]{2,0,1:T(8,128)(2,1)} async-done(((bf16[160,16,2048]{2,0,1:T(8,128)(2,1)}), bf16[160,16,2048]{2,0,1:T(8,128)(2,1)}, u32[]{:S(2)}, u32[]{:S(2)}) %all-to-all-start) | async-done | bytes 10485792 | tf_op jit(solution)/shard_map/all_to_all | solution.py:26
  222.6 9.9 %convolution_bitcast_fusion = f32[2560,512]{0,1:T(8,128)S(1)} fusion(bf16[2560,2048]{1,0:T(8,128)(2,1)} %bitcast.10, bf16[2048,512]{1,0:T(8,128)(2,1)} %all-gather.2.cloned.1.call-done, pred[2048]{0:T(1024)(128)(4,1)S(1)} %iota_compare_fusion.3), kind=kOutput, calls=%fused_computation.8 | convolution fusion | flops 5369757696 | bytes 17827840 | tf_op jit(solution)/shard_map/dot_general | solution.py:30
  232.5 0.6 collective-permute-start
  233.1 112.7 %collective-permute-done = f32[2560,512]{0,1:T(8,128)S(1)} collective-permute-done((f32[2560,512]{0,1:T(8,128)S(1)}, f32[2560,512]{0,1:T(8,128)S(1)}, u32[]{:S(2)}, u32[]{:S(2)}) %collective-permute-start) | collective-permute-done | bytes 5242912 | tf_op jit(solution)/shard_map/ppermute | solution.py:33
  345.9 0.9 add.60
  346.8 14.3 %collective-permute-start.1 = (f32[2560,512]{0,1:T(8,128)S(1)}, f32[2560,512]{0,1:T(8,128)S(1)}, u32[]{:S(2)}, u32[]{:S(2)}) collective-permute-start(f32[2560,512]{0,1:T(8,128)S(1)} %add.60), channel_id=1, source_target_pairs={{0,4},{2,6},{4,0},{6,2},{8,12},{10,14},{12,8},{14,10},{16,20},{18,... | collective-permute-start | bytes 15728648 | tf_op jit(solution)/shard_map/ppermute | solution.py:33
  361.1 110.3 %collective-permute-done.1 = f32[2560,512]{0,1:T(8,128)S(1)} collective-permute-done((f32[2560,512]{0,1:T(8,128)S(1)}, f32[2560,512]{0,1:T(8,128)S(1)}, u32[]{:S(2)}, u32[]{:S(2)}) %collective-permute-start.1) | collective-permute-done | bytes 5242912 | tf_op jit(solution)/shard_map/ppermute | solution.py:33
  471.4 3.3 add.61
  474.7 29.7 %collective-permute-start.2 = (f32[2560,512]{0,1:T(8,128)}, f32[2560,512]{0,1:T(8,128)}, u32[]{:S(2)}, u32[]{:S(2)}) collective-permute-start(f32[2560,512]{0,1:T(8,128)} %add.61), channel_id=1, source_target_pairs={{0,8},{2,10},{4,12},{6,14},{8,0},{10,2},{12,4},{14,6},{16,24},{18,... | collective-permute-start | bytes 15728648 | tf_op jit(solution)/shard_map/ppermute | solution.py:33
  504.4 2.8 fusion.28
  507.2 131.4 %collective-permute-done.2 = f32[2560,512]{0,1:T(8,128)} collective-permute-done((f32[2560,512]{0,1:T(8,128)}, f32[2560,512]{0,1:T(8,128)}, u32[]{:S(2)}, u32[]{:S(2)}) %collective-permute-start.2) | collective-permute-done | bytes 5242912 | tf_op jit(solution)/shard_map/ppermute | solution.py:33
  638.6 7.3 add.62
  645.9 2.3 collective-permute-start.3
  648.3 1.6 copy.12
  649.9 0.2 fusion.27
  650.2 11.7 %cholesky.104 = f32[128,128]{1,0:T(8,128)S(1)} custom-call(f32[128,128]{1,0:T(8,128)S(1)} %cholesky.266), custom_call_target="Cholesky" | custom-call | tf_op jit(solution)/shard_map/jit(cholesky)/cholesky | solution.py:28
  661.9 0.1 cholesky.224
  662.0 9.8 %custom-call.32 = f32[1,128,128]{1,2,0:T(8,128)S(1)} custom-call(f32[1,128,128]{2,1,0:T(8,128)S(1)} %get-tuple-element.32), custom_call_target="InvertDiagBlocksLowerTriangular" | custom-call | tf_op jit(solution)/shard_map/jit(cholesky)/cholesky | solution.py:28
  671.9 0.3 constant_dynamic-update-slice_fusion
  672.2 0.5 convolution_subtract_fusion.2
  672.7 11.7 %cholesky.217 = f32[128,128]{1,0:T(8,128)S(1)} custom-call(f32[128,128]{1,0:T(8,128)S(1)} %cholesky.270), custom_call_target="Cholesky" | custom-call | tf_op jit(solution)/shard_map/jit(cholesky)/cholesky | solution.py:28
  684.5 9.8 %custom-call.33 = f32[1,128,128]{1,2,0:T(8,128)S(1)} custom-call(f32[1,128,128]{2,1,0:T(8,128)S(1)} %get-tuple-element.29), custom_call_target="InvertDiagBlocksLowerTriangular" | custom-call | tf_op jit(solution)/shard_map/jit(cholesky)/cholesky | solution.py:28
  694.3 0.3 convolution_dynamic-update-slice_fusion
  694.6 0.4 convolution_subtract_fusion.3
  695.0 11.7 %cholesky.238 = f32[128,128]{1,0:T(8,128)S(1)} custom-call(f32[128,128]{1,0:T(8,128)S(1)} %cholesky.275), custom_call_target="Cholesky" | custom-call | tf_op jit(solution)/shard_map/jit(cholesky)/cholesky | solution.py:28
  706.7 10.2 %custom-call.34 = f32[1,128,128]{1,2,0:T(8,128)S(1)} custom-call(f32[1,128,128]{2,1,0:T(8,128)S(1)} %get-tuple-element.26), custom_call_target="InvertDiagBlocksLowerTriangular" | custom-call | tf_op jit(solution)/shard_map/jit(cholesky)/cholesky | solution.py:28
  716.9 0.2 convolution_dynamic-update-slice_fusion.1
  717.1 0.4 convolution_subtract_fusion.4
  717.5 11.7 %cholesky.255 = f32[128,128]{1,0:T(8,128)S(1)} custom-call(f32[128,128]{1,0:T(8,128)S(1)} %convolution_subtract_fusion.4), custom_call_target="Cholesky" | custom-call | tf_op jit(solution)/shard_map/jit(cholesky)/cholesky | solution.py:28
  729.2 0.7 compare_reduce_fusion.2
  731.1 0.7 compare_reduce_fusion.1
  732.5 0.7 compare_reduce_fusion
  733.9 0.1 select_select_fusion
  734.1 7.9 while.1
  734.2 0.6 fusion.71
  734.7 1.3 bitcast_dynamic-update-slice_fusion.2
  736.1 0.6 fusion.71
  736.7 1.3 bitcast_dynamic-update-slice_fusion.2
  738.1 0.6 fusion.71
  738.7 1.3 bitcast_dynamic-update-slice_fusion.2
  740.1 0.6 fusion.71
  740.7 1.3 bitcast_dynamic-update-slice_fusion.2
  742.0 39.5 %custom-call.35 = f32[4,128,128]{1,2,0:T(8,128)S(1)} custom-call(f32[4,128,128]{2,1,0:T(8,128)S(1)} %get-tuple-element.12), custom_call_target="InvertDiagBlocksLowerTriangular" | custom-call | tf_op jit(solution)/shard_map/triangular_solve | solution.py:10
  781.5 89.8 %collective-permute-done.3 = f32[2560,512]{0,1:T(8,128)} collective-permute-done((f32[2560,512]{0,1:T(8,128)}, f32[2560,512]{0,1:T(8,128)}, u32[]{:S(2)}, u32[]{:S(2)}) %collective-permute-start.3) | collective-permute-done | bytes 5242912 | tf_op jit(solution)/shard_map/ppermute | solution.py:33
  871.3 5.0 add_bitcast_fusion
  876.3 1.3 fusion.25
  877.5 1.3 fusion.44
  878.8 1.3 fusion.24
  880.1 1.5 fusion.15
  881.6 1.3 fusion.23
  882.9 2.5 fusion
  885.4 1.3 fusion.22
  886.7 1.5 fusion.54
  888.1 1.3 convolution_subtract_fusion
  889.4 1.3 fusion.53
  890.7 1.6 convolution_subtract_fusion.1
  892.3 1.3 fusion.52
  893.5 2.5 fusion.12
  896.0 1.3 fusion.51
  897.3 0.8 fusion.32
  (23 shorter events, 0.6 us)
Async XLA Ops:
  16.6 206.0 %all-to-all-start = ((bf16[160,16,2048]{2,0,1:T(8,128)(2,1)}), bf16[160,16,2048]{2,0,1:T(8,128)(2,1)}, u32[]{:S(2)}, u32[]{:S(2)}) async-start(bf16[160,16,2048]{2,0,1:T(8,128)(2,1)} %bitcast.68), calls=%async_computation | async-start | bytes 20971520 | tf_op jit(solution)/shard_map/all_to_all | solution.py:26
  24.9 14.0 %all-gather.2.cloned.1.call-start = ((), (), s32[]{:S(2)}) async-start(), calls=%async_computation.1 | async-start | bytes 3145728 | tf_op jit(solution)/shard_map/all_gather | solution.py:17
  25.7 622.6 %all-reduce.3.cloned.1.call-start = ((), (), s32[]{:S(2)}) async-start(), calls=%async_computation.2 | async-start | bytes 2097152 | tf_op jit(solution)/shard_map/psum | solution.py:27
  232.5 113.4 %collective-permute-start = (f32[2560,512]{0,1:T(8,128)S(1)}, f32[2560,512]{0,1:T(8,128)S(1)}, u32[]{:S(2)}, u32[]{:S(2)}) collective-permute-start(f32[2560,512]{0,1:T(8,128)S(1)} %convolution_bitcast_fusion), channel_id=1, source_target_pairs={{0,2},{2,0},{4,6},{6,4},{8,10},{10,8},{12,14},{14,12},{16,18},{18,... | collective-permute-start | bytes 15728648 | tf_op jit(solution)/shard_map/ppermute | solution.py:33
  346.8 157.6 %copy-start.1 = (bf16[2048,512]{1,0:T(8,128)(2,1)S(1)}, bf16[2048,512]{1,0:T(8,128)(2,1)}, u32[]{:S(2)}) copy-start(bf16[2048,512]{1,0:T(8,128)(2,1)} %all-gather.2.cloned.1.call-done) | copy-start | bytes 6291460
  346.8 124.6 %collective-permute-start.1 = (f32[2560,512]{0,1:T(8,128)S(1)}, f32[2560,512]{0,1:T(8,128)S(1)}, u32[]{:S(2)}, u32[]{:S(2)}) collective-permute-start(f32[2560,512]{0,1:T(8,128)S(1)} %add.60), channel_id=1, source_target_pairs={{0,4},{2,6},{4,0},{6,2},{8,12},{10,14},{12,8},{14,10},{16,20},{18,... | collective-permute-start | bytes 15728648 | tf_op jit(solution)/shard_map/ppermute | solution.py:33
  474.7 163.9 %collective-permute-start.2 = (f32[2560,512]{0,1:T(8,128)}, f32[2560,512]{0,1:T(8,128)}, u32[]{:S(2)}, u32[]{:S(2)}) collective-permute-start(f32[2560,512]{0,1:T(8,128)} %add.61), channel_id=1, source_target_pairs={{0,8},{2,10},{4,12},{6,14},{8,0},{10,2},{12,4},{14,6},{16,24},{18,... | collective-permute-start | bytes 15728648 | tf_op jit(solution)/shard_map/ppermute | solution.py:33
  645.9 225.4 %collective-permute-start.3 = (f32[2560,512]{0,1:T(8,128)}, f32[2560,512]{0,1:T(8,128)}, u32[]{:S(2)}, u32[]{:S(2)}) collective-permute-start(f32[2560,512]{0,1:T(8,128)} %add.62), channel_id=1, source_target_pairs={{0,16},{2,18},{4,20},{6,22},{8,24},{10,26},{12,28},{14,30},{16,0},... | collective-permute-start | bytes 15728648 | tf_op jit(solution)/shard_map/ppermute | solution.py:33
  648.3 1.7 copy-start
Sparse Core Ops, SparseCore 0:
  27.3 11.5 all-gather.1
  507.3 123.3 all-reduce.2
